TPU v7x, 256 devices: a whole 4x4x8 slice. The times are simulated.
256 devices in a mesh: row: 16 (over x, y_lo, core), col: 8 (over z), slab: 2 (over y_hi).
Axes of the slice: x: 4, y: 4 (y_hi: 2, y_lo: 2; y = y_hi * 2 + y_lo), z: 8, core: 2. Of those that a mesh axis runs over, the one named last changes fastest.
Arguments:
- fields: bfloat16 [2, 16384, 1024], P(None, ('row', 'col', 'slab')), may hold values from -0.8984375 to 0.8984375
Outputs:
- gram: float32 [2, 16384, 16384], P(None, ('row', 'slab'), 'col')
All inputs are finite; a program needn't handle non-finite values.
Results may differ from a plain program's by a relative error of at most 0.01.
Values may be sent and summed in bfloat16 or wider, within the bound.
A program may use at most 64 MiB of HBM per device.

v0:
```python
import jax
import jax.numpy as jnp
from jax import lax
from jax.sharding import PartitionSpec as P


def pair_terms(left_real, left_imag, piece):
    right_real = jnp.concatenate([piece[0], piece[1]], axis=1)
    right_imag = jnp.concatenate([piece[1], piece[0]], axis=1)
    dims = (((1,), (1,)), ((), ()))
    real = lax.dot_general(left_real, right_real, dims, preferred_element_type=jnp.float32)
    imag = lax.dot_general(left_imag, right_imag, dims, preferred_element_type=jnp.float32)
    return jnp.stack([real, imag])


def body(fields):
    local = lax.all_to_all(fields, "slab", split_axis=2, concat_axis=1, tiled=True)
    row_block = lax.all_gather(local, "col", axis=1, tiled=True)
    left_real = jnp.concatenate([row_block[0], row_block[1]], axis=1)
    left_imag = jnp.concatenate([row_block[0], -row_block[1]], axis=1)
    column_set = lax.all_gather(local, "row", axis=1, tiled=True)
    terms = pair_terms(left_real, left_imag, column_set)
    gram = lax.psum_scatter(
        terms.astype(jnp.bfloat16), "slab", scatter_dimension=1, tiled=True
    ).astype(jnp.float32)
    return gram


def solution(mesh):
    placed = (P(None, ("row", "col", "slab"), None),)
    return jax.shard_map(
        body, mesh=mesh, in_specs=placed, out_specs=P(None, ("row", "slab"), "col"), check_vma=False
    )
```

profile of v0, /device:TPU:1, one launch (start us, length us, event | category | flops | bytes accessed | tf_op | source)
XLA Modules:
  0.0 242.6 jit_solution(3190334933049715580)
XLA Ops:
  6.5 0.0 all-gather.3.cloned.1.call-start
  6.5 1.3 copy.3
  7.8 0.4 reshape
  8.2 10.3 %all_to_all.18 = bf16[2,2,32768]{2,1,0:T(2,128)(2,1)S(1)} all-to-all(bf16[2,2,32768]{2,1,0:T(2,128)(2,1)S(1)} %reshape), channel_id=1, replica_groups=mesh['row'=16,'col'=8,'slab'=2] {'slab'}, dimensions={0} | all-to-all | bytes 524288 | tf_op jit(solution)/shard_map/all_to_all | solution.py:17
  18.6 0.3 reshape.1
  18.9 1.0 copy.5
  19.9 0.0 all-gather.3.cloned.1.call-update
  19.9 0.0 all-gather.5.cloned.1.call-start
  20.0 0.7 all-gather.5.cloned.1.call-update
  20.7 0.0 reduce-scatter.2.cloned.1.call-start
  20.7 38.7 %all-gather.3.cloned.1.call-done = bf16[2,1024,512]{2,1,0:T(8,128)(2,1)} async-done(((bf16[2,128,512]{2,1,0:T(8,128)(2,1)}), bf16[2,1024,512]{2,1,0:T(8,128)(2,1)}) %all-gather.3.cloned.1.call-update) | async-done | bytes 2097168 | tf_op jit(solution)/shard_map/all_gather | solution.py:18
  59.4 1.3 fusion.16
  60.7 2.6 %slice_bitcast_fusion.2 = (bf16[1024,512]{1,0:T(8,128)(2,1)}, bf16[1024,512]{1,0:T(8,128)(2,1)S(1)}) fusion(bf16[2,1024,512]{2,1,0:T(8,128)(2,1)} %all-gather.3.cloned.1.call-done), kind=kLoop, calls=%fused_computation.17 | loop fusion | bytes 4194304 | tf_op jit(solution)/shard_map/squeeze | solution.py:19
  63.3 40.4 %all-gather.5.cloned.1.call-done = bf16[2,2048,512]{2,1,0:T(8,128)(2,1)} async-done(((bf16[2,128,512]{2,1,0:T(8,128)(2,1)}), bf16[2,2048,512]{2,1,0:T(8,128)(2,1)}) %all-gather.5.cloned.1.call-update) | async-done | bytes 4194320 | tf_op jit(solution)/shard_map/all_gather | solution.py:21
  103.8 0.0 copy-start
  103.8 2.6 %slice_bitcast_fusion = (bf16[2048,512]{1,0:T(8,128)(2,1)S(1)}, bf16[2048,512]{1,0:T(8,128)(2,1)S(1)}) fusion(bf16[2,2048,512]{2,1,0:T(8,128)(2,1)} %all-gather.5.cloned.1.call-done), kind=kLoop, calls=%fused_computation.13 | loop fusion | bytes 8388608 | tf_op jit(solution)/shard_map/squeeze | solution.py:8
  106.3 0.0 copy-done
  106.3 4.8 %convert_bitcast_fusion.1 = bf16[1,1024,2048]{2,1,0:T(8,128)(2,1)S(1)} fusion(bf16[2048,512]{1,0:T(8,128)(2,1)S(1)} %get-tuple-element.5, bf16[2048,512]{1,0:T(8,128)(2,1)S(1)} %get-tuple-element.6, bf16[1024,512]{1,0:T(8,128)(2,1)S(1)} %get-tuple-element.8, bf16[1024,512]{1,0:T(8,128)(2,1)S(1)} %copy-done), kind=kOutput, calls=%fused_computation.10 | convolution fusion | flops 4309647360 | bytes 10485760 | tf_op jit(solution)/shard_map/dot_general | solution.py:11
  111.1 6.1 %convert_bitcast_fusion = bf16[1,1024,2048]{2,1,0:T(8,128)(2,1)} fusion(bf16[2048,512]{1,0:T(8,128)(2,1)S(1)} %get-tuple-element.6, bf16[2048,512]{1,0:T(8,128)(2,1)S(1)} %get-tuple-element.5, bf16[1024,512]{1,0:T(8,128)(2,1)S(1)} %get-tuple-element.8, bf16[1024,512]{1,0:T(8,128)(2,1)S(1)} %fusion.16), kind=kOutput, calls=%fused_computation.9 | convolution fusion | flops 4309647360 | bytes 10485760 | tf_op jit(solution)/shard_map/dot_general | solution.py:12
  117.3 6.3 %pad_maximum_fusion = bf16[2,1024,2048]{2,1,0:T(8,128)(2,1)} fusion(bf16[1,1024,2048]{2,1,0:T(8,128)(2,1)} %convert_bitcast_fusion, bf16[1,1024,2048]{2,1,0:T(8,128)(2,1)S(1)} %convert_bitcast_fusion.1), kind=kLoop, calls=%fused_computation | loop fusion | flops 4194304 | bytes 16777216 | tf_op jit(solution)/shard_map/stack | solution.py:13
  123.6 0.0 reduce-scatter.2.cloned.1.call-update
  123.6 105.7 %reduce-scatter.2.cloned.1.call-done = bf16[2,512,2048]{2,1,0:T(8,128)(2,1)} async-done(((bf16[2,1024,2048]{2,1,0:T(8,128)(2,1)}), bf16[2,512,2048]{2,1,0:T(8,128)(2,1)}) %reduce-scatter.2.cloned.1.call-update) | async-done | bytes 4194320 | tf_op jit(solution)/shard_map/reduce_scatter | solution.py:23
  229.4 6.7 %convert_element_type.4 = f32[2,512,2048]{2,1,0:T(8,128)} convert(bf16[2,512,2048]{2,1,0:T(8,128)(2,1)} %reduce-scatter.2.cloned.1.call-done) | non-fusion elementwise | flops 2097152 | bytes 12582912 | tf_op jit(solution)/shard_map/convert_element_type | solution.py:25
Async XLA Ops:
  6.5 52.9 %all-gather.3.cloned.1.call-start = ((), (), s32[]{:S(2)}) async-start(), calls=%async_computation.2 | async-start | bytes 2359296 | tf_op jit(solution)/shard_map/all_gather | solution.py:18
  19.9 83.8 %all-gather.5.cloned.1.call-start = ((), (), s32[]{:S(2)}) async-start(), calls=%async_computation.3 | async-start | bytes 4456448 | tf_op jit(solution)/shard_map/all_gather | solution.py:21
  20.7 208.7 %reduce-scatter.2.cloned.1.call-start = ((), (), s32[]{:S(2)}) async-start(), calls=%async_computation.4 | async-start | bytes 12582912 | tf_op jit(solution)/shard_map/reduce_scatter | solution.py:23
  103.8 2.6 %copy-start = (bf16[1024,512]{1,0:T(8,128)(2,1)S(1)}, bf16[1024,512]{1,0:T(8,128)(2,1)}, u32[]{:S(2)}) copy-start(bf16[1024,512]{1,0:T(8,128)(2,1)} %get-tuple-element.7) | copy-start | bytes 3145732
Sparse Core Ops, SparseCore 0:
  20.1 39.2 all-gather.2
  61.2 42.4 all-gather.4
  123.8 105.5 reduce-scatter.1
where the time goes:
time: 243 us
  waiting for transfers between devices  186 us (77%)
  other arithmetic  14.3 us (6%)
  between operations  13.2 us (5%)
  matrix products  10.9 us (4%)
  blocking collectives  10.3 us (4%)
  local copies, waits for them, and re-layouts  8.25 us (3%)
    reduce_scatter x1, waiting for transfers between devices, body(): lax.psum_scatter(terms.astype(jnp.bfloat16), 'slab', scatter_dimension=1,...  106 us
    all_gather x1, waiting for transfers between devices, body(): column_set = lax.all_gather(local, 'row', axis=1, tiled=True)  40.4 us
    all_gather x1, waiting for transfers between devices, body(): row_block = lax.all_gather(local, 'col', axis=1, tiled=True)  38.7 us
    all_to_all x1, blocking collectives, body(): lax.all_to_all(fields, 'slab', split_axis=2, concat_axis=1, tiled=True)  10.3 us
    convert_element_type x1, other arithmetic, body(): gram = lax.psum_scatter(terms.astype(jnp.bfloat16), 'slab', scatter_dimen...  6.65 us
    another operation x1, other arithmetic, pair_terms(): return jnp.stack([real, imag])  6.35 us
    dot_general x1, matrix products, pair_terms(): lax.dot_general(left_imag, right_imag, dims, preferred_element_type=jnp.f...  6.13 us
  transfers between devices with their start and end apart: 3, of which 3 were waited for; matrix products, arithmetic and copies ran while one was open for 2% of the time, Pallas kernels for 0%

commit v1 on v0

--- a/solution.py
+++ b/solution.py
@@ -18,7 +18,9 @@
     row_block = lax.all_gather(local, "col", axis=1, tiled=True)
     left_real = jnp.concatenate([row_block[0], row_block[1]], axis=1)
     left_imag = jnp.concatenate([row_block[0], -row_block[1]], axis=1)
-    column_set = lax.all_gather(local, "row", axis=1, tiled=True)
+    column_set = jnp.concatenate(
+        lax.all_to_all(jnp.stack([local] * lax.axis_size("row")), "row", 0, 0), axis=1
+    )
     terms = pair_terms(left_real, left_imag, column_set)
     gram = lax.psum_scatter(
         terms.astype(jnp.bfloat16), "slab", scatter_dimension=1, tiled=True

time: 243 us -> 229 us (0.942)
  waiting for transfers between devices: 186 us -> 162 us
  starting transfers between devices: 0.08 us -> 6.57 us
  local copies, waits for them, and re-layouts: 8.25 us -> 11.7 us
    all_gather x1 -> x0, waiting for transfers between devices: 40.4 us -> none  [body(): column_set = lax.all_gather(local, 'row', axis=1, tiled=True)]
    all_to_all x0 -> x1, waiting for transfers between devices: none -> 19.3 us  [body(): lax.all_to_all(jnp.stack([local] * lax.axis_size('row')), 'row', 0, 0)]
    all_gather x1, waiting for transfers between devices: 38.7 us -> 29.4 us  [body(): row_block = lax.all_gather(local, 'col', axis=1, tiled=True)]
    reduce_scatter x1, waiting for transfers between devices: 106 us -> 113 us  [body(): lax.psum_scatter(terms.astype(jnp.bfloat16), 'slab', scatter_dimension=1,...]
    all_to_all x0 -> x1, starting transfers between devices: none -> 6.53 us  [body(): lax.all_to_all(jnp.stack([local] * lax.axis_size('row')), 'row', 0, 0)]
    another operation x0 -> x1, local copies, waits for them, and re-layouts: none -> 3.44 us  [body(): jnp.stack([local] * lax.axis_size('row'))]
    slice x0 -> x1, local copies, waits for them, and re-layouts: none -> 2.58 us  [pair_terms(): right_real = jnp.concatenate([piece[0], piece[1]], axis=1)]
    squeeze x1 -> x0, local copies, waits for them, and re-layouts: 2.58 us -> none  [pair_terms(): right_real = jnp.concatenate([piece[0], piece[1]], axis=1)]
  transfers between devices with their start and end apart: 3 -> 3, of which waited for: 3 -> 3; matrix products, arithmetic and copies ran while one was open for 2% -> 3% of each run, Pallas kernels for 0% -> 0%
where the time goes in v1:
time: 229 us
  waiting for transfers between devices  162 us (71%)
  other arithmetic  14.3 us (6%)
  between operations  13.4 us (6%)
  local copies, waits for them, and re-layouts  11.7 us (5%)
  matrix products  10.9 us (5%)
  blocking collectives  10.3 us (4%)
  starting transfers between devices  6.57 us (3%)
    reduce_scatter x1, waiting for transfers between devices, body(): lax.psum_scatter(terms.astype(jnp.bfloat16), 'slab', scatter_dimension=1,...  113 us
    all_gather x1, waiting for transfers between devices, body(): row_block = lax.all_gather(local, 'col', axis=1, tiled=True)  29.4 us
    all_to_all x1, waiting for transfers between devices, body(): lax.all_to_all(jnp.stack([local] * lax.axis_size('row')), 'row', 0, 0)  19.3 us
    all_to_all x1, blocking collectives, body(): lax.all_to_all(fields, 'slab', split_axis=2, concat_axis=1, tiled=True)  10.3 us
    convert_element_type x1, other arithmetic, body(): gram = lax.psum_scatter(terms.astype(jnp.bfloat16), 'slab', scatter_dimen...  6.65 us
    all_to_all x1, starting transfers between devices, body(): lax.all_to_all(jnp.stack([local] * lax.axis_size('row')), 'row', 0, 0)  6.53 us
    another operation x1, other arithmetic, pair_terms(): return jnp.stack([real, imag])  6.35 us
    dot_general x1, matrix products, pair_terms(): lax.dot_general(left_real, right_real, dims, preferred_element_type=jnp.f...  6.11 us
  transfers between devices with their start and end apart: 3, of which 3 were waited for; matrix products, arithmetic and copies ran while one was open for 3% of the time, Pallas kernels for 0%

profile of v1, /device:TPU:1, one launch (start us, length us, event | category | flops | bytes accessed | tf_op | source)
XLA Modules:
  0.0 228.8 jit_solution(15045254659983773219)
XLA Ops:
  6.5 0.0 all-gather.2.cloned.1.call-start
  6.5 1.3 copy.3
  7.8 0.4 reshape.12
  8.2 10.3 %all_to_all.23 = bf16[2,2,32768]{2,1,0:T(2,128)(2,1)S(1)} all-to-all(bf16[2,2,32768]{2,1,0:T(2,128)(2,1)S(1)} %reshape.12), channel_id=1, replica_groups=mesh['row'=16,'col'=8,'slab'=2] {'slab'}, dimensions={0} | all-to-all | bytes 524288 | tf_op jit(solution)/shard_map/all_to_all | solution.py:17
  18.6 0.3 reshape.13
  18.9 1.0 copy.5
  19.9 0.0 all-gather.2.cloned.1.call-update
  20.0 3.4 %stack.11 = bf16[16,2,128,512]{3,2,1,0:T(8,128)(2,1)} broadcast(bf16[2,128,512]{2,1,0:T(8,128)(2,1)} %bitcast.21), dimensions={1,2,3} | broadcast | bytes 4456448 | tf_op jit(solution)/shard_map/stack | solution.py:22
  23.4 6.5 %all-to-all-start.1 = ((bf16[16,2,128,512]{3,2,1,0:T(8,128)(2,1)}), bf16[16,2,128,512]{3,2,1,0:T(8,128)(2,1)}, u32[]{:S(2)}, u32[]{:S(2)}) async-start(bf16[16,2,128,512]{3,2,1,0:T(8,128)(2,1)} %stack.11), calls=%async_computation.1 | async-start | bytes 8388608 | tf_op jit(solution)/shard_map/all_to_all | solution.py:22
  29.9 0.0 reduce-scatter.2.cloned.1.call-start
  30.0 29.4 %all-gather.2.cloned.1.call-done = bf16[2,1024,512]{2,1,0:T(8,128)(2,1)} async-done(((bf16[2,128,512]{2,1,0:T(8,128)(2,1)}), bf16[2,1024,512]{2,1,0:T(8,128)(2,1)}) %all-gather.2.cloned.1.call-update) | async-done | bytes 2097168 | tf_op jit(solution)/shard_map/all_gather | solution.py:18
  59.4 1.3 fusion.16
  60.7 2.7 %slice_bitcast_fusion = (bf16[1024,512]{1,0:T(8,128)(2,1)S(1)}, bf16[1024,512]{1,0:T(8,128)(2,1)}) fusion(bf16[2,1024,512]{2,1,0:T(8,128)(2,1)} %all-gather.2.cloned.1.call-done), kind=kLoop, calls=%fused_computation.15 | loop fusion | bytes 4194304 | tf_op jit(solution)/shard_map/squeeze | solution.py:19
  63.4 19.3 %all-to-all-done.1 = bf16[16,2,128,512]{3,2,1,0:T(8,128)(2,1)} async-done(((bf16[16,2,128,512]{3,2,1,0:T(8,128)(2,1)}), bf16[16,2,128,512]{3,2,1,0:T(8,128)(2,1)}, u32[]{:S(2)}, u32[]{:S(2)}) %all-to-all-start.1) | async-done | bytes 4194336 | tf_op jit(solution)/shard_map/all_to_all | solution.py:22
  82.6 0.0 copy-start
  82.6 2.6 %fusion.17 = (bf16[1,16,128,512]{3,2,0,1:T(8,128)(2,1)S(1)}, bf16[1,16,128,512]{3,2,0,1:T(8,128)(2,1)S(1)}) fusion(bf16[2,16,128,512]{3,2,0,1:T(8,128)(2,1)} %bitcast.7), kind=kLoop, calls=%fused_computation.20 | loop fusion | bytes 8388608 | tf_op jit(solution)/shard_map/slice | solution.py:8
  85.2 0.0 copy-done
  85.2 4.8 %convert_bitcast_fusion = bf16[1,1024,2048]{2,1,0:T(8,128)(2,1)S(1)} fusion(bf16[2048,512]{1,0:T(8,128)(2,1)S(1)} %bitcast.26, bf16[2048,512]{1,0:T(8,128)(2,1)S(1)} %bitcast.24, bf16[1024,512]{1,0:T(8,128)(2,1)S(1)} %copy-done, bf16[1024,512]{1,0:T(8,128)(2,1)S(1)} %fusion.16), kind=kOutput, calls=%fused_computation.9 | convolution fusion | flops 4309647360 | bytes 10485760 | tf_op jit(solution)/shard_map/dot_general | solution.py:12
  90.0 6.1 %convert_bitcast_fusion.1 = bf16[1,1024,2048]{2,1,0:T(8,128)(2,1)} fusion(bf16[2048,512]{1,0:T(8,128)(2,1)S(1)} %bitcast.25, bf16[2048,512]{1,0:T(8,128)(2,1)S(1)} %bitcast.27, bf16[1024,512]{1,0:T(8,128)(2,1)S(1)} %copy-done, bf16[1024,512]{1,0:T(8,128)(2,1)S(1)} %get-tuple-element.7), kind=kOutput, calls=%fused_computation.10 | convolution fusion | flops 4309647360 | bytes 10485760 | tf_op jit(solution)/shard_map/dot_general | solution.py:11
  96.1 6.3 %pad_maximum_fusion = bf16[2,1024,2048]{2,1,0:T(8,128)(2,1)} fusion(bf16[1,1024,2048]{2,1,0:T(8,128)(2,1)S(1)} %convert_bitcast_fusion, bf16[1,1024,2048]{2,1,0:T(8,128)(2,1)} %convert_bitcast_fusion.1), kind=kLoop, calls=%fused_computation | loop fusion | flops 4194304 | bytes 16777216 | tf_op jit(solution)/shard_map/stack | solution.py:13
  102.5 0.0 reduce-scatter.2.cloned.1.call-update
  102.5 112.8 %reduce-scatter.2.cloned.1.call-done = bf16[2,512,2048]{2,1,0:T(8,128)(2,1)} async-done(((bf16[2,1024,2048]{2,1,0:T(8,128)(2,1)}), bf16[2,512,2048]{2,1,0:T(8,128)(2,1)}) %reduce-scatter.2.cloned.1.call-update) | async-done | bytes 4194320 | tf_op jit(solution)/shard_map/reduce_scatter | solution.py:25
  215.3 6.7 %convert_element_type.4 = f32[2,512,2048]{2,1,0:T(8,128)} convert(bf16[2,512,2048]{2,1,0:T(8,128)(2,1)} %reduce-scatter.2.cloned.1.call-done) | non-fusion elementwise | flops 2097152 | bytes 12582912 | tf_op jit(solution)/shard_map/convert_element_type | solution.py:27
Async XLA Ops:
  6.5 52.9 %all-gather.2.cloned.1.call-start = ((), (), s32[]{:S(2)}) async-start(), calls=%async_computation.3 | async-start | bytes 2359296 | tf_op jit(solution)/shard_map/all_gather | solution.py:18
  23.4 59.3 %all-to-all-start.1 = ((bf16[16,2,128,512]{3,2,1,0:T(8,128)(2,1)}), bf16[16,2,128,512]{3,2,1,0:T(8,128)(2,1)}, u32[]{:S(2)}, u32[]{:S(2)}) async-start(bf16[16,2,128,512]{3,2,1,0:T(8,128)(2,1)} %stack.11), calls=%async_computation.1 | async-start | bytes 8388608 | tf_op jit(solution)/shard_map/all_to_all | solution.py:22
  29.9 185.4 %reduce-scatter.2.cloned.1.call-start = ((), (), s32[]{:S(2)}) async-start(), calls=%async_computation.4 | async-start | bytes 12582912 | tf_op jit(solution)/shard_map/reduce_scatter | solution.py:25
  82.6 2.6 %copy-start = (bf16[1024,512]{1,0:T(8,128)(2,1)S(1)}, bf16[1024,512]{1,0:T(8,128)(2,1)}, u32[]{:S(2)}) copy-start(bf16[1024,512]{1,0:T(8,128)(2,1)} %get-tuple-element.8) | copy-start | bytes 3145732
Sparse Core Ops, SparseCore 0:
  20.1 39.2 all-gather.1
  102.6 112.6 reduce-scatter.1
